TPU v7x, 512 devices: a whole 4x8x8 slice. The times are simulated.
512 devices in a mesh: dp: 4 (over x_lo, core), blk: 128 (over y, z, x_hi).
Axes of the slice: x: 4 (x_hi: 2, x_lo: 2; x = x_hi * 2 + x_lo), y: 8, z: 8, core: 2. Of those that a mesh axis runs over, the one named last changes fastest.
Arguments:
- queries: bfloat16 [4, 24576, 512], P('dp', 'blk'), may hold values from -6 to 6, as said below
- key_in: bfloat16 [4, 24576, 512], P('dp', 'blk'), may hold values from -6 to 6, as said below
- value_in: bfloat16 [4, 24576, 512], P('dp', 'blk'), may hold values from -6 to 6
- out_weight: bfloat16 [512, 1024], replicated, may hold values from -2 to 2
- conv_kernel: float32 [31, 1024], replicated, may hold values from -1 to 1
- cotangent: bfloat16 [4, 24576, 1024], P('dp', 'blk'), may hold values from -6 to 6
Outputs:
- out_frames: bfloat16 [4, 24576, 1024], P('dp', 'blk')
- query_grad: bfloat16 [4, 24576, 512], P('dp', 'blk')
- key_grad: bfloat16 [4, 24576, 512], P('dp', 'blk')
- value_grad: bfloat16 [4, 24576, 512], P('dp', 'blk')
- weight_grad: float32 [512, 1024], replicated
- kernel_grad: float32 [31, 1024], replicated
Inputs may be any that keep to these rules, and one draw needn't show every extreme that they name: `queries`: independent entries. `key_in`: independent entries.
All inputs are finite; a program needn't handle non-finite values.
Results may differ from a plain program's by a relative error of at most 0.024.
Values may be sent and summed in bfloat16 or wider, within the bound.
A program may use at most 64 MiB of HBM per device.

v0:
```python
import math
import jax
import jax.numpy as jnp
from jax import lax
from jax.sharding import PartitionSpec as P

ATT_HEADS = 8
HEAD_DIM = 64
CTX_MAX = 3
ATT = 512
NEGATIVE = -1e30


def from_behind(block, axis, distance):
    devices = range(lax.axis_size(axis))
    route = [(i - distance, i) for i in devices if i - distance in devices]
    return lax.ppermute(block, axis, route)


def split_heads(matrix):
    return matrix.reshape(matrix.shape[0], ATT_HEADS, HEAD_DIM)


def tile_scores(query_heads, tile, query_pos, key_pos, usable, left_span, score_scale):
    key_heads = split_heads(tile[:, :ATT])
    scores = (
        jnp.einsum("qhd,khd->hqk", query_heads, key_heads, preferred_element_type=jnp.float32)
        * score_scale
    )
    distance = query_pos[:, None] - key_pos[None, :]
    visible = ((distance >= 0) & (distance < left_span) & usable)[None]
    return (jnp.where(visible, scores, NEGATIVE), visible)


def attend_tile(
    softmax_state, query_heads, tile, query_pos, key_pos, usable, left_span, score_scale
):
    running_max, running_sum, weighted = softmax_state
    scores, visible = tile_scores(
        query_heads, tile, query_pos, key_pos, usable, left_span, score_scale
    )
    new_max = jnp.maximum(running_max, jnp.max(scores, axis=-1))
    weights = jnp.where(visible, jnp.exp(scores - new_max[..., None]), 0.0)
    fading = jnp.exp(running_max - new_max)
    running_sum = running_sum * fading + jnp.sum(weights, axis=-1)
    value_heads = split_heads(tile[:, ATT:])
    update = jnp.einsum(
        "hqk,khd->qhd",
        weights.astype(jnp.bfloat16),
        value_heads,
        preferred_element_type=jnp.float32,
    )
    weighted = weighted * jnp.transpose(fading)[:, :, None] + update
    return (new_max, running_sum, weighted)


def tile_grads(
    query_heads,
    dout_heads,
    log_sums,
    deltas,
    tile,
    query_pos,
    key_pos,
    usable,
    left_span,
    score_scale,
):
    scores, visible = tile_scores(
        query_heads, tile, query_pos, key_pos, usable, left_span, score_scale
    )
    key_heads = split_heads(tile[:, :ATT])
    value_heads = split_heads(tile[:, ATT:])
    probs = jnp.where(visible, jnp.exp(scores - log_sums[..., None]), 0.0)
    dvalue_heads = jnp.einsum(
        "hqk,qhd->khd", probs.astype(jnp.bfloat16), dout_heads, preferred_element_type=jnp.float32
    )
    dprobs = jnp.einsum("qhd,khd->hqk", dout_heads, value_heads, preferred_element_type=jnp.float32)
    dscores = (probs * (dprobs - deltas[..., None])).astype(jnp.bfloat16)
    dquery = (
        jnp.einsum("hqk,khd->qhd", dscores, key_heads, preferred_element_type=jnp.float32)
        * score_scale
    )
    dkey_heads = (
        jnp.einsum("hqk,qhd->khd", dscores, query_heads, preferred_element_type=jnp.float32)
        * score_scale
    )
    row_count = tile.shape[0]
    return (
        dquery,
        jnp.concatenate(
            [dkey_heads.reshape(row_count, ATT), dvalue_heads.reshape(row_count, ATT)], axis=1
        ),
    )


def depthwise(extended, conv_kernel, row_count, ahead):
    tap_count = conv_kernel.shape[0]

    def add_tap(tap_index, running):
        first_row = tap_index if ahead else tap_count - 1 - tap_index
        return running + conv_kernel[tap_index] * lax.dynamic_slice_in_dim(
            extended, first_row, row_count, 0
        )

    empty = jnp.zeros((row_count, extended.shape[1]), jnp.float32)
    return lax.fori_loop(0, tap_count, add_tap, empty)


def sum_weights(weight_part, kernel_part):
    return lax.psum((weight_part, kernel_part), ("dp", "blk"))


def per_device(queries, key_in, value_in, out_weight, conv_kernel, cotangent):
    cycle_count = lax.axis_size("blk")
    device = lax.axis_index("blk")
    row_count = queries.shape[1]
    context = min(CTX_MAX, cycle_count // 4)
    left_span = context * row_count
    score_scale = 1.0 / math.sqrt(HEAD_DIM)
    edge_rows = conv_kernel.shape[0] - 1
    row_ids = jnp.arange(row_count, dtype=jnp.int32)
    query_heads = split_heads(queries[0])
    own_tile = jnp.concatenate([key_in[0], value_in[0]], axis=1)
    own_pos = device * row_count + row_ids
    always = jnp.array(True)

    def source(offset):
        anchor = device - offset
        return (anchor * row_count + row_ids, anchor >= 0)

    start_state = (
        jnp.full((ATT_HEADS, row_count), NEGATIVE, jnp.float32),
        jnp.zeros((ATT_HEADS, row_count), jnp.float32),
        jnp.zeros((row_count, ATT_HEADS, HEAD_DIM), jnp.float32),
    )
    first_state = attend_tile(
        start_state, query_heads, own_tile, own_pos, own_pos, always, left_span, score_scale
    )

    def forward_step(carry, offset):
        moving, softmax_state = carry
        arrived = from_behind(moving, "blk", 1)
        tile_pos, tile_usable = source(offset)
        softmax_state = attend_tile(
            softmax_state,
            query_heads,
            arrived,
            own_pos,
            tile_pos,
            tile_usable,
            left_span,
            score_scale,
        )
        return ((arrived, softmax_state), arrived)

    offsets = jnp.arange(1, context + 1, dtype=jnp.int32)
    (unused_tile, final_state), kept_tiles = lax.scan(
        forward_step, (own_tile, first_state), offsets
    )
    running_max, running_sum, weighted = final_state
    attended = (weighted / jnp.transpose(running_sum)[:, :, None]).astype(jnp.bfloat16)
    log_sums = running_max + jnp.log(running_sum)
    flat = attended.reshape(row_count, ATT)
    hidden = jnp.dot(flat, out_weight, preferred_element_type=jnp.float32).astype(jnp.bfloat16)
    before = from_behind(hidden[-edge_rows:], "blk", 1)
    extended = jnp.concatenate([before, hidden], axis=0).astype(jnp.float32)
    mixed = depthwise(extended, conv_kernel, row_count, False)
    sigma = jax.nn.sigmoid(mixed)
    out_frames = (mixed * sigma).astype(jnp.bfloat16)[None]
    upstream = cotangent[0].astype(jnp.float32)
    dmixed = upstream * sigma * (1.0 + mixed * (1.0 - sigma))
    after = from_behind(dmixed[:edge_rows].astype(jnp.bfloat16), "blk", -1).astype(jnp.float32)
    dextended = jnp.concatenate([dmixed, after], axis=0)
    dhidden = depthwise(dextended, conv_kernel, row_count, True).astype(jnp.bfloat16)

    def kernel_tap(tap_index):
        window = lax.dynamic_slice_in_dim(extended, edge_rows - tap_index, row_count, 0)
        return jnp.sum(dmixed * window, axis=0)

    kernel_part = lax.map(kernel_tap, jnp.arange(edge_rows + 1, dtype=jnp.int32))
    weight_part = jnp.einsum("ra,rd->ad", flat, dhidden, preferred_element_type=jnp.float32)
    dattended = jnp.einsum(
        "rd,ad->ra", dhidden, out_weight, preferred_element_type=jnp.float32
    ).astype(jnp.bfloat16)
    dout_heads = split_heads(dattended)
    deltas = jnp.einsum("rhe,rhe->hr", dout_heads, attended, preferred_element_type=jnp.float32)
    dquery_own, dkv_own = tile_grads(
        query_heads,
        dout_heads,
        log_sums,
        deltas,
        own_tile,
        own_pos,
        own_pos,
        always,
        left_span,
        score_scale,
    )
    zero_buffer = jnp.zeros((row_count, 2 * ATT), jnp.float32)

    def backward_step(carry, inputs):
        buffer, dquery_sum = carry
        tile, offset = inputs
        tile_pos, tile_usable = source(offset)
        dquery_part, dkv_part = tile_grads(
            query_heads,
            dout_heads,
            log_sums,
            deltas,
            tile,
            own_pos,
            tile_pos,
            tile_usable,
            left_span,
            score_scale,
        )
        arrived = from_behind((buffer + dkv_part).astype(jnp.bfloat16), "blk", -1).astype(
            jnp.float32
        )
        return ((arrived, dquery_sum + dquery_part), None)

    (buffer, dquery_sum), unused = lax.scan(
        backward_step, (zero_buffer, dquery_own), (kept_tiles, offsets), reverse=True
    )
    dkv_total = dkv_own + buffer
    weight_total, kernel_total = sum_weights(weight_part, kernel_part)
    query_grad = dquery_sum.reshape(row_count, ATT).astype(jnp.bfloat16)[None]
    key_grad = dkv_total[:, :ATT].astype(jnp.bfloat16)[None]
    value_grad = dkv_total[:, ATT:].astype(jnp.bfloat16)[None]
    return (out_frames, query_grad, key_grad, value_grad, weight_total, kernel_total)


def solution(mesh):
    return jax.shard_map(
        per_device,
        mesh=mesh,
        in_specs=(
            P("dp", "blk", None),
            P("dp", "blk", None),
            P("dp", "blk", None),
            P(),
            P(),
            P("dp", "blk", None),
        ),
        out_specs=(
            P("dp", "blk", None),
            P("dp", "blk", None),
            P("dp", "blk", None),
            P("dp", "blk", None),
            P(),
            P(),
        ),
        check_vma=False,
    )
```

profile of v0, /device:TPU:24, one launch (start us, length us, event | category | flops | bytes accessed | tf_op | source)
XLA Modules:
  0.0 622.3 jit_solution(3382806898935224929)
XLA Ops:
  12.4 69.9 %while.79 = (s32[]{:T(128)}, bf16[192,1024]{0,1:T(8,128)(2,1)S(1)}, f32[8,192]{1,0:T(8,128)S(1)}, f32[8,192]{1,0:T(8,128)S(1)}, f32[192,8,64]{0,2,1:T(8,128)S(1)...) while((s32[]{:T(128)}, bf16[192,1024]{0,1:T(8,128)(2,1)S(1)}, ...), condition=%wide.region_5.6_spmd.clone, body=%wide.region_2.5_spmd.clone.sunk | while | flops 78537600 | bytes 9227495 | solution.py:158
  12.4 4.9 collective-permute-start
  18.7 18.9 %collective-permute-done = bf16[192,1024]{0,1:T(8,128)(2,1)S(1)} collective-permute-done((bf16[192,1024]{0,1:T(8,128)(2,1)S(1)}, bf16[192,1024]{0,1:T(8,128)(2,1)S(1)}, u32[]{:S(2)}, u32[]{:S(2)}) %collective-permute-start) | collective-permute-done | bytes 393248 | tf_op jit(solution)/shard_map/while/body/eval_jaxpr/ppermute | solution.py:17
  39.8 1.9 collective-permute-start
  43.1 16.2 %collective-permute-done = bf16[192,1024]{0,1:T(8,128)(2,1)S(1)} collective-permute-done((bf16[192,1024]{0,1:T(8,128)(2,1)S(1)}, bf16[192,1024]{0,1:T(8,128)(2,1)S(1)}, u32[]{:S(2)}, u32[]{:S(2)}) %collective-permute-start) | collective-permute-done | bytes 393248 | tf_op jit(solution)/shard_map/while/body/eval_jaxpr/ppermute | solution.py:17
  61.5 1.9 collective-permute-start
  64.8 15.3 %collective-permute-done = bf16[192,1024]{0,1:T(8,128)(2,1)S(1)} collective-permute-done((bf16[192,1024]{0,1:T(8,128)(2,1)S(1)}, bf16[192,1024]{0,1:T(8,128)(2,1)S(1)}, u32[]{:S(2)}, u32[]{:S(2)}) %collective-permute-start) | collective-permute-done | bytes 393248 | tf_op jit(solution)/shard_map/while/body/eval_jaxpr/ppermute | solution.py:17
  82.8 1.9 collective-permute-start.2
  84.9 8.7 %collective-permute-done.2 = bf16[30,1024]{1,0:T(8,128)(2,1)S(1)} collective-permute-done((bf16[30,1024]{1,0:T(8,128)(2,1)S(1)}, bf16[30,1024]{1,0:T(8,128)(2,1)S(1)}, u32[]{:S(2)}, u32[]{:S(2)}) %collective-permute-start.2) | collective-permute-done | bytes 61472 | tf_op jit(solution)/shard_map/ppermute | solution.py:17
  94.6 36.2 %while.80 = (s32[]{:T(128)}, f32[192,1024]{1,0:T(8,128)S(1)}, f32[31,1024]{1,0:T(8,128)}, f32[222,1024]{1,0:T(8,128)S(1)}, s32[]{:T(128)}, /*index=5*/s32[]{:T(128)}, s32[]{:T(128)}, s32[]{:T(128)}) while((s32[]{:T(128)}, f32[192,1024]{1,0:T(8,128)S(1)}, f32[31,1024]{1,0:T(8,128)}, f32[222,1024]{1,0:T(8,128)S(1)}, s32[]{:T(128)}, ...), condition=%wide.region_7.8_spmd.clone, body=%wide.region_6.7_spmd.clone.sunk | while | flops 589831 | bytes 2371741 | solution.py:107
  131.7 2.3 fusion.39
  134.1 1.9 collective-permute-start.3
  136.0 106.3 %while.78 = (s32[]{:T(128)}, f32[31,1024]{1,0:T(8,128)}, s32[31]{0:T(128)S(1)}, f32[222,1024]{1,0:T(8,128)S(1)}, f32[192,1024]{1,0:T(8,128)S(1)}, /*index=5*/s32[]{:T(128)}, s32[1]{0:T(128)}, s32[]{:T(128)}, s32[1]{0:T(128)}) while((s32[]{:T(128)}, f32[31,1024]{1,0:T(8,128)}, s32[31]{0:T(128)S(1)}, f32[222,1024]{1,0:T(8,128)S(1)}, ...), condition=%wide.region_15.16_spmd, body=%wide.region_13.15_spmd.sunk | while | flops 392198 | bytes 1585319 | solution.py:181
  243.8 71.2 %while.81 = (s32[]{:T(128)}, f32[192,1024]{1,0:T(8,128)S(1)}, f32[31,1024]{1,0:T(8,128)}, f32[222,1024]{1,0:T(8,128)}, s32[]{:T(128)}, /*index=5*/s32[]{:T(128)}) while((s32[]{:T(128)}, f32[192,1024]{1,0:T(8,128)S(1)}, f32[31,1024]{1,0:T(8,128)}, f32[222,1024]{1,0:T(8,128)}, s32[]{:T(128)}, /*index=5*/s32[]{:T(128)}) %tuple.190), condition=%wide.region_9.10_spmd.clone, body=%wide.region_8.9_spmd.clone.sunk | while | flops 589827 | bytes 2371679 | solution.py:107
  244.6 1.5 select_add_fusion.5
  246.9 1.5 select_add_fusion.5
  256.1 1.5 select_add_fusion.5
  258.4 1.5 select_add_fusion.5
  315.9 2.4 convolution_convert_fusion.1
  324.2 1.8 fusion.48
  328.3 63.4 %while.82 = (s32[]{:T(128)}, f32[192,1024]{0,1:T(8,128)S(1)}, f32[192,8,64]{0,2,1:T(8,128)}, s32[3]{0:T(128)S(1)}, s32[]{:T(128)}, /*index=5*/bf16[3,192,1024]{1...) while((s32[]{:T(128)}, f32[192,1024]{0,1:T(8,128)S(1)}, ...), condition=%wide.region_11.12_spmd.clone, body=%wide.region_10.11_spmd.clone.sunk | while | flops 192565632 | bytes 15424801 | solution.py:223
  333.5 1.9 collective-permute-start.1
  335.4 2.2 fusion.139
  337.6 10.0 %collective-permute-done.1 = bf16[192,1024]{0,1:T(8,128)(2,1)} collective-permute-done((bf16[192,1024]{0,1:T(8,128)(2,1)}, bf16[192,1024]{0,1:T(8,128)(2,1)}, u32[]{:S(2)}, u32[]{:S(2)}) %collective-permute-start.1) | collective-permute-done | bytes 393248 | tf_op jit(solution)/shard_map/while/body/eval_jaxpr/ppermute | solution.py:17
  354.1 5.3 collective-permute-start.1
  359.4 2.2 fusion.139
  361.6 6.5 %collective-permute-done.1 = bf16[192,1024]{0,1:T(8,128)(2,1)} collective-permute-done((bf16[192,1024]{0,1:T(8,128)(2,1)}, bf16[192,1024]{0,1:T(8,128)(2,1)}, u32[]{:S(2)}, u32[]{:S(2)}) %collective-permute-start.1) | collective-permute-done | bytes 393248 | tf_op jit(solution)/shard_map/while/body/eval_jaxpr/ppermute | solution.py:17
  374.5 8.4 %collective-permute-start.1 = (bf16[192,1024]{0,1:T(8,128)(2,1)}, bf16[192,1024]{0,1:T(8,128)(2,1)}, u32[]{:S(2)}, u32[]{:S(2)}) collective-permute-start(bf16[192,1024]{0,1:T(8,128)(2,1)} %fusion.138), channel_id=1, source_target_pairs={{1,0},{2,1},{3,2},{4,3},{5,4},{6,5},{7,6},{8,7},{9,8},{10,9},{11,1... | collective-permute-start | bytes 1179656 | tf_op jit(solution)/shard_map/while/body/eval_jaxpr/ppermute | solution.py:17
  382.9 2.2 fusion.139
  385.1 5.4 collective-permute-done.1
  395.8 215.8 %all-reduce.3.cloned.1.call-done = (f32[512,1024]{1,0:T(8,128)}, f32[31,1024]{1,0:T(8,128)}) async-done(((f32[512,1024]{1,0:T(8,128)}, f32[31,1024]{1,0:T(8,128)}), (f32[512,1024]{1,0:T(8,128)}, f32[31,1024]{1,0:T(8,128)})) %all-reduce.3.cloned.1.call-update) | async-done | bytes 2224144 | tf_op jit(solution)/shard_map/psum | solution.py:111
  611.6 3.2 copy.121
  (363 shorter events, 214.3 us)
Async XLA Ops:
  7.2 75.2 %copy-start = (bf16[512,1024]{1,0:T(8,128)(2,1)S(1)}, bf16[512,1024]{1,0:T(8,128)(2,1)}, u32[]{:S(2)}) copy-start(bf16[512,1024]{1,0:T(8,128)(2,1)} %param.19) | copy-start | bytes 3145732
  7.2 604.5 %all-reduce.3.cloned.1.call-start = ((), (), s32[]{:S(2)}) async-start(), calls=%async_computation | async-start | bytes 4456448 | tf_op jit(solution)/shard_map/psum | solution.py:111
  8.6 3.1 copy-start.10
  11.3 1.1 copy-start.1
  12.4 25.2 %collective-permute-start = (bf16[192,1024]{0,1:T(8,128)(2,1)S(1)}, bf16[192,1024]{0,1:T(8,128)(2,1)S(1)}, u32[]{:S(2)}, u32[]{:S(2)}) collective-permute-start(bf16[192,1024]{0,1:T(8,128)(2,1)S(1)} %get-tuple-element.1015), channel_id=1, source_target_pairs={{0,1},{1,2},{2,3},{3,4},{4,5},{5,6},{6,7},{7,8},{8,9},{9,10},{10,1... | collective-permute-start | bytes 1179656 | tf_op jit(solution)/shard_map/while/body/eval_jaxpr/ppermute | solution.py:17
  39.8 19.5 %collective-permute-start = (bf16[192,1024]{0,1:T(8,128)(2,1)S(1)}, bf16[192,1024]{0,1:T(8,128)(2,1)S(1)}, u32[]{:S(2)}, u32[]{:S(2)}) collective-permute-start(bf16[192,1024]{0,1:T(8,128)(2,1)S(1)} %get-tuple-element.1015), channel_id=1, source_target_pairs={{0,1},{1,2},{2,3},{3,4},{4,5},{5,6},{6,7},{7,8},{8,9},{9,10},{10,1... | collective-permute-start | bytes 1179656 | tf_op jit(solution)/shard_map/while/body/eval_jaxpr/ppermute | solution.py:17
  61.5 18.6 %collective-permute-start = (bf16[192,1024]{0,1:T(8,128)(2,1)S(1)}, bf16[192,1024]{0,1:T(8,128)(2,1)S(1)}, u32[]{:S(2)}, u32[]{:S(2)}) collective-permute-start(bf16[192,1024]{0,1:T(8,128)(2,1)S(1)} %get-tuple-element.1015), channel_id=1, source_target_pairs={{0,1},{1,2},{2,3},{3,4},{4,5},{5,6},{6,7},{7,8},{8,9},{9,10},{10,1... | collective-permute-start | bytes 1179656 | tf_op jit(solution)/shard_map/while/body/eval_jaxpr/ppermute | solution.py:17
  82.3 2.5 copy-start.7
  82.4 2.5 copy-start.12
  82.8 2.0 copy-start.15
  82.8 10.7 %collective-permute-start.2 = (bf16[30,1024]{1,0:T(8,128)(2,1)S(1)}, bf16[30,1024]{1,0:T(8,128)(2,1)S(1)}, u32[]{:S(2)}, u32[]{:S(2)}) collective-permute-start(bf16[30,1024]{1,0:T(8,128)(2,1)S(1)} %slice.52), channel_id=1, source_target_pairs={{0,1},{1,2},{2,3},{3,4},{4,5},{5,6},{6,7},{7,8},{8,9},{9,10},{10,1... | collective-permute-start | bytes 184328 | tf_op jit(solution)/shard_map/ppermute | solution.py:17
  130.9 0.9 copy-start.8
  134.1 108.3 %collective-permute-start.3 = (bf16[30,1024]{1,0:T(8,128)(2,1)S(1)}, bf16[30,1024]{1,0:T(8,128)(2,1)S(1)}, u32[]{:S(2)}, u32[]{:S(2)}) collective-permute-start(bf16[30,1024]{1,0:T(8,128)(2,1)S(1)} %slice.59), channel_id=1, source_target_pairs={{1,0},{2,1},{3,2},{4,3},{5,4},{6,5},{7,6},{8,7},{9,8},{10,9},{11,1... | collective-permute-start | bytes 184328 | tf_op jit(solution)/shard_map/ppermute | solution.py:17
  242.4 1.5 copy-start.3
  315.0 0.9 copy-start.4
  315.9 4.6 copy-start.2
  321.8 0.9 copy-start.11
  322.7 1.4 copy-start.5
  322.7 1.4 copy-start.13
  324.2 1.8 copy-start.14
  326.9 1.4 copy-start.6
  330.6 0.8 copy-start.9
  333.5 14.1 %collective-permute-start.1 = (bf16[192,1024]{0,1:T(8,128)(2,1)}, bf16[192,1024]{0,1:T(8,128)(2,1)}, u32[]{:S(2)}, u32[]{:S(2)}) collective-permute-start(bf16[192,1024]{0,1:T(8,128)(2,1)} %fusion.138), channel_id=1, source_target_pairs={{1,0},{2,1},{3,2},{4,3},{5,4},{6,5},{7,6},{8,7},{9,8},{10,9},{11,1... | collective-permute-start | bytes 1179656 | tf_op jit(solution)/shard_map/while/body/eval_jaxpr/ppermute | solution.py:17
  351.2 0.8 copy-start.9
  354.1 14.0 %collective-permute-start.1 = (bf16[192,1024]{0,1:T(8,128)(2,1)}, bf16[192,1024]{0,1:T(8,128)(2,1)}, u32[]{:S(2)}, u32[]{:S(2)}) collective-permute-start(bf16[192,1024]{0,1:T(8,128)(2,1)} %fusion.138), channel_id=1, source_target_pairs={{1,0},{2,1},{3,2},{4,3},{5,4},{6,5},{7,6},{8,7},{9,8},{10,9},{11,1... | collective-permute-start | bytes 1179656 | tf_op jit(solution)/shard_map/while/body/eval_jaxpr/ppermute | solution.py:17
  371.6 0.8 copy-start.9
  374.5 16.0 %collective-permute-start.1 = (bf16[192,1024]{0,1:T(8,128)(2,1)}, bf16[192,1024]{0,1:T(8,128)(2,1)}, u32[]{:S(2)}, u32[]{:S(2)}) collective-permute-start(bf16[192,1024]{0,1:T(8,128)(2,1)} %fusion.138), channel_id=1, source_target_pairs={{1,0},{2,1},{3,2},{4,3},{5,4},{6,5},{7,6},{8,7},{9,8},{10,9},{11,1... | collective-permute-start | bytes 1179656 | tf_op jit(solution)/shard_map/while/body/eval_jaxpr/ppermute | solution.py:17
  611.6 3.2 copy-start.16
Sparse Core Ops, SparseCore 0:
  328.0 283.6 all-reduce.2
where the time goes:
time: 632 us; the launch traced here: 622 us
  waiting for transfers between devices  297 us (47%)
  local copies, waits for them, and re-layouts  134 us (21%)
  other arithmetic  79.2 us (13%)
  loops' own time  46.3 us (7%)
  starting transfers between devices  28.2 us (4%)
  matrix products  23.3 us (4%)
  between operations  14.4 us (2%)
    psum x1, waiting for transfers between devices, sum_weights(): return lax.psum((weight_part, kernel_part), ('dp', 'blk'))  216 us
    ppermute x8, waiting for transfers between devices, from_behind(): return lax.ppermute(block, axis, route)  81.1 us
    add x62, other arithmetic, add_tap(): running + conv_kernel[tap_index] * lax.dynamic_slice_in_dim(extended, fir...  58.3 us
    dynamic_slice x62, local copies, waits for them, and re-layouts, add_tap(): conv_kernel[tap_index]  47.7 us
    dynamic_update_slice x31, local copies, waits for them, and re-layouts, per_device(): lax.map(kernel_tap, jnp.arange(edge_rows + 1, dtype=jnp.int32))  43.4 us
    another operation x1, loops' own time, per_device(): lax.map(kernel_tap, jnp.arange(edge_rows + 1, dtype=jnp.int32))  40.4 us
    ppermute x8, starting transfers between devices, from_behind(): return lax.ppermute(block, axis, route)  28.1 us
    dynamic_slice x31, local copies, waits for them, and re-layouts, per_device(): lax.map(kernel_tap, jnp.arange(edge_rows + 1, dtype=jnp.int32))  18 us
  transfers between devices with their start and end apart: 9, of which 8 were waited for; matrix products, arithmetic and copies ran while one was open for 15% of the time, Pallas kernels for 0%

commit v1 on v0

--- a/solution.py
+++ b/solution.py
@@ -108,7 +108,7 @@
 
 
 def sum_weights(weight_part, kernel_part):
-    return lax.psum((weight_part, kernel_part), ("dp", "blk"))
+    return lax.psum(lax.psum((weight_part, kernel_part), "dp"), "blk")
 
 
 def per_device(queries, key_in, value_in, out_weight, conv_kernel, cotangent):

time: 632 us -> 1760 us (2.78)
  the two profiles are of different devices: /device:TPU:24 before, /device:TPU:32 now
where the time goes in v1:
time: 1760 us; the launch traced here: 1750 us
  waiting for transfers between devices  1410 us (80%)
  local copies, waits for them, and re-layouts  134 us (8%)
  other arithmetic  79.1 us (4%)
  loops' own time  46.3 us (3%)
  starting transfers between devices  41 us (2%)
  matrix products  24.5 us (1%)
    psum x2, waiting for transfers between devices, sum_weights(): return lax.psum(lax.psum((weight_part, kernel_part), 'dp'), 'blk')  1320 us
    ppermute x8, waiting for transfers between devices, from_behind(): return lax.ppermute(block, axis, route)  89.7 us
    add x62, other arithmetic, add_tap(): running + conv_kernel[tap_index] * lax.dynamic_slice_in_dim(extended, fir...  58.3 us
    dynamic_slice x62, local copies, waits for them, and re-layouts, add_tap(): conv_kernel[tap_index]  47.7 us
    dynamic_update_slice x31, local copies, waits for them, and re-layouts, per_device(): lax.map(kernel_tap, jnp.arange(edge_rows + 1, dtype=jnp.int32))  43.4 us
    ppermute x8, starting transfers between devices, from_behind(): return lax.ppermute(block, axis, route)  40.9 us
    another operation x1, loops' own time, per_device(): lax.map(kernel_tap, jnp.arange(edge_rows + 1, dtype=jnp.int32))  40.4 us
  transfers between devices with their start and end apart: 10, of which 9 were waited for; matrix products, arithmetic and copies ran while one was open for 6% of the time, Pallas kernels for 0%

profile of v1, /device:TPU:32, one launch (start us, length us, event | category | flops | bytes accessed | tf_op | source)
XLA Modules:
  0.0 1746.4 jit_solution(14839362597210874129)
XLA Ops:
  12.4 72.3 %while.79 = (s32[]{:T(128)}, bf16[192,1024]{0,1:T(8,128)(2,1)S(1)}, f32[8,192]{1,0:T(8,128)S(1)}, f32[8,192]{1,0:T(8,128)S(1)}, f32[192,8,64]{0,2,1:T(8,128)S(1)...) while((s32[]{:T(128)}, bf16[192,1024]{0,1:T(8,128)(2,1)S(1)}, ...), condition=%wide.region_5.6_spmd.clone, body=%wide.region_2.5_spmd.clone.sunk | while | flops 78537600 | bytes 9227495 | solution.py:158
  12.4 4.9 collective-permute-start
  18.7 18.9 %collective-permute-done = bf16[192,1024]{0,1:T(8,128)(2,1)S(1)} collective-permute-done((bf16[192,1024]{0,1:T(8,128)(2,1)S(1)}, bf16[192,1024]{0,1:T(8,128)(2,1)S(1)}, u32[]{:S(2)}, u32[]{:S(2)}) %collective-permute-start) | collective-permute-done | bytes 393248 | tf_op jit(solution)/shard_map/while/body/eval_jaxpr/ppermute | solution.py:17
  39.8 1.9 collective-permute-start
  43.1 17.4 collective-permute-done
  62.7 1.9 collective-permute-start
  66.0 16.5 collective-permute-done
  85.2 1.9 collective-permute-start.2
  87.2 9.9 collective-permute-done.2
  98.2 36.2 %while.80 = (s32[]{:T(128)}, f32[192,1024]{1,0:T(8,128)S(1)}, f32[31,1024]{1,0:T(8,128)}, f32[222,1024]{1,0:T(8,128)S(1)}, s32[]{:T(128)}, /*index=5*/s32[]{:T(128)}, s32[]{:T(128)}, s32[]{:T(128)}) while((s32[]{:T(128)}, f32[192,1024]{1,0:T(8,128)S(1)}, f32[31,1024]{1,0:T(8,128)}, f32[222,1024]{1,0:T(8,128)S(1)}, s32[]{:T(128)}, ...), condition=%wide.region_7.8_spmd.clone, body=%wide.region_6.7_spmd.clone.sunk | while | flops 589831 | bytes 2371741 | solution.py:107
  135.4 2.3 fusion.39
  137.7 1.9 collective-permute-start.3
  139.6 106.3 %while.78 = (s32[]{:T(128)}, f32[31,1024]{1,0:T(8,128)}, s32[31]{0:T(128)S(1)}, f32[222,1024]{1,0:T(8,128)S(1)}, f32[192,1024]{1,0:T(8,128)S(1)}, /*index=5*/s32[]{:T(128)}, s32[1]{0:T(128)}, s32[]{:T(128)}, s32[1]{0:T(128)}) while((s32[]{:T(128)}, f32[31,1024]{1,0:T(8,128)}, s32[31]{0:T(128)S(1)}, f32[222,1024]{1,0:T(8,128)S(1)}, ...), condition=%wide.region_16.17_spmd, body=%wide.region_14.16_spmd.sunk | while | flops 392198 | bytes 1585319 | solution.py:181
  247.4 71.2 %while.81 = (s32[]{:T(128)}, f32[192,1024]{1,0:T(8,128)S(1)}, f32[31,1024]{1,0:T(8,128)}, f32[222,1024]{1,0:T(8,128)}, s32[]{:T(128)}, /*index=5*/s32[]{:T(128)}) while((s32[]{:T(128)}, f32[192,1024]{1,0:T(8,128)S(1)}, f32[31,1024]{1,0:T(8,128)}, f32[222,1024]{1,0:T(8,128)}, s32[]{:T(128)}, /*index=5*/s32[]{:T(128)}) %tuple.193), condition=%wide.region_9.10_spmd.clone, body=%wide.region_8.9_spmd.clone.sunk | while | flops 589827 | bytes 2371679 | solution.py:107
  248.2 1.5 select_add_fusion.5
  318.6 1.8 fusion.48
  320.5 2.4 convolution_convert_fusion.1
  325.2 2.0 copy.51
  331.1 2.3 fusion.33
  333.4 53.9 %all-reduce.7.cloned.1.call-done = (f32[512,1024]{1,0:T(8,128)}, f32[31,1024]{1,0:T(8,128)}) async-done(((f32[512,1024]{1,0:T(8,128)}, f32[31,1024]{1,0:T(8,128)}), (f32[512,1024]{1,0:T(8,128)}, f32[31,1024]{1,0:T(8,128)})) %all-reduce.7.cloned.1.call-update) | async-done | bytes 2224144 | tf_op jit(solution)/shard_map/psum | solution.py:111
  387.4 81.2 %while.82 = (s32[]{:T(128)}, f32[192,1024]{0,1:T(8,128)S(1)}, f32[192,8,64]{0,2,1:T(8,128)}, s32[3]{0:T(128)S(1)}, s32[]{:T(128)}, /*index=5*/bf16[3,192,1024]{1...) while((s32[]{:T(128)}, f32[192,1024]{0,1:T(8,128)S(1)}, ...), condition=%wide.region_11.12_spmd.clone, body=%wide.region_10.11_spmd.clone.sunk | while | flops 192565632 | bytes 15424801 | solution.py:223
  392.6 8.0 collective-permute-start.1
  400.6 2.2 fusion.139
  402.8 10.0 collective-permute-done.1
  419.2 10.2 collective-permute-start.1
  429.4 2.2 fusion.139
  431.6 8.9 collective-permute-done.1
  446.9 10.2 collective-permute-start.1
  457.1 2.2 fusion.139
  459.3 8.1 collective-permute-done.1
  472.7 1263.0 %all-reduce.5.cloned.1.call-done = (f32[512,1024]{1,0:T(8,128)}, f32[31,1024]{1,0:T(8,128)}) async-done(((f32[512,1024]{1,0:T(8,128)}, f32[31,1024]{1,0:T(8,128)}), (f32[512,1024]{1,0:T(8,128)}, f32[31,1024]{1,0:T(8,128)})) %all-reduce.5.cloned.1.call-update) | async-done | bytes 2224144 | tf_op jit(solution)/shard_map/psum | solution.py:111
  1735.7 3.2 copy.123
  (364 shorter events, 216.2 us)
Async XLA Ops:
  7.2 77.6 %copy-start = (bf16[512,1024]{1,0:T(8,128)(2,1)S(1)}, bf16[512,1024]{1,0:T(8,128)(2,1)}, u32[]{:S(2)}) copy-start(bf16[512,1024]{1,0:T(8,128)(2,1)} %param.19) | copy-start | bytes 3145732
  7.2 380.1 %all-reduce.7.cloned.1.call-start = ((), (), s32[]{:S(2)}) async-start(), calls=%async_computation.1 | async-start | bytes 4456448 | tf_op jit(solution)/shard_map/psum | solution.py:111
  8.6 3.1 copy-start.10
  11.3 1.1 copy-start.1
  12.4 25.2 %collective-permute-start = (bf16[192,1024]{0,1:T(8,128)(2,1)S(1)}, bf16[192,1024]{0,1:T(8,128)(2,1)S(1)}, u32[]{:S(2)}, u32[]{:S(2)}) collective-permute-start(bf16[192,1024]{0,1:T(8,128)(2,1)S(1)} %get-tuple-element.1017), channel_id=1, source_target_pairs={{0,1},{1,2},{2,3},{3,4},{4,5},{5,6},{6,7},{7,8},{8,9},{9,10},{10,1... | collective-permute-start | bytes 1179656 | tf_op jit(solution)/shard_map/while/body/eval_jaxpr/ppermute | solution.py:17
  39.8 20.7 %collective-permute-start = (bf16[192,1024]{0,1:T(8,128)(2,1)S(1)}, bf16[192,1024]{0,1:T(8,128)(2,1)S(1)}, u32[]{:S(2)}, u32[]{:S(2)}) collective-permute-start(bf16[192,1024]{0,1:T(8,128)(2,1)S(1)} %get-tuple-element.1017), channel_id=1, source_target_pairs={{0,1},{1,2},{2,3},{3,4},{4,5},{5,6},{6,7},{7,8},{8,9},{9,10},{10,1... | collective-permute-start | bytes 1179656 | tf_op jit(solution)/shard_map/while/body/eval_jaxpr/ppermute | solution.py:17
  62.7 19.8 %collective-permute-start = (bf16[192,1024]{0,1:T(8,128)(2,1)S(1)}, bf16[192,1024]{0,1:T(8,128)(2,1)S(1)}, u32[]{:S(2)}, u32[]{:S(2)}) collective-permute-start(bf16[192,1024]{0,1:T(8,128)(2,1)S(1)} %get-tuple-element.1017), channel_id=1, source_target_pairs={{0,1},{1,2},{2,3},{3,4},{4,5},{5,6},{6,7},{7,8},{8,9},{9,10},{10,1... | collective-permute-start | bytes 1179656 | tf_op jit(solution)/shard_map/while/body/eval_jaxpr/ppermute | solution.py:17
  84.7 2.5 copy-start.6
  84.8 2.4 copy-start.12
  85.2 2.0 copy-start.14
  85.2 11.9 collective-permute-start.2
  134.5 0.9 copy-start.7
  137.7 108.2 %collective-permute-start.3 = (bf16[30,1024]{1,0:T(8,128)(2,1)S(1)}, bf16[30,1024]{1,0:T(8,128)(2,1)S(1)}, u32[]{:S(2)}, u32[]{:S(2)}) collective-permute-start(bf16[30,1024]{1,0:T(8,128)(2,1)S(1)} %slice.59), channel_id=1, source_target_pairs={{1,0},{2,1},{3,2},{4,3},{5,4},{6,5},{7,6},{8,7},{9,8},{10,9},{11,1... | collective-permute-start | bytes 184328 | tf_op jit(solution)/shard_map/ppermute | solution.py:17
  245.9 1.5 copy-start.3
  247.4 71.2 %copy-start.13 = (bf16[192,8,64]{0,2,1:T(8,128)(2,1)S(1)}, bf16[192,8,64]{0,2,1:T(8,128)(2,1)}, u32[]{:S(2)}) copy-start(bf16[192,8,64]{0,2,1:T(8,128)(2,1)} %copy-done.12) | copy-start | bytes 589828
  318.6 1.8 copy-start.4
  320.4 3.6 copy-start.2
  320.4 1415.3 %all-reduce.5.cloned.1.call-start = ((), (), s32[]{:S(2)}) async-start(), calls=%async_computation | async-start | bytes 4456448 | tf_op jit(solution)/shard_map/psum | solution.py:111
  328.9 0.9 copy-start.9
  329.8 1.4 copy-start.11
  331.1 56.2 %copy-start.5 = (f32[192,1024]{0,1:T(8,128)S(1)}, f32[192,1024]{0,1:T(8,128)}, u32[]{:S(2)}) copy-start(f32[192,1024]{0,1:T(8,128)} %custom-call.2) | copy-start | bytes 2359300
  389.7 0.8 copy-start.8
  392.6 20.1 %collective-permute-start.1 = (bf16[192,1024]{0,1:T(8,128)(2,1)}, bf16[192,1024]{0,1:T(8,128)(2,1)}, u32[]{:S(2)}, u32[]{:S(2)}) collective-permute-start(bf16[192,1024]{0,1:T(8,128)(2,1)} %fusion.138), channel_id=1, source_target_pairs={{1,0},{2,1},{3,2},{4,3},{5,4},{6,5},{7,6},{8,7},{9,8},{10,9},{11,1... | collective-permute-start | bytes 1179656 | tf_op jit(solution)/shard_map/while/body/eval_jaxpr/ppermute | solution.py:17
  416.3 0.8 copy-start.8
  419.2 21.3 %collective-permute-start.1 = (bf16[192,1024]{0,1:T(8,128)(2,1)}, bf16[192,1024]{0,1:T(8,128)(2,1)}, u32[]{:S(2)}, u32[]{:S(2)}) collective-permute-start(bf16[192,1024]{0,1:T(8,128)(2,1)} %fusion.138), channel_id=1, source_target_pairs={{1,0},{2,1},{3,2},{4,3},{5,4},{6,5},{7,6},{8,7},{9,8},{10,9},{11,1... | collective-permute-start | bytes 1179656 | tf_op jit(solution)/shard_map/while/body/eval_jaxpr/ppermute | solution.py:17
  444.0 0.8 copy-start.8
  446.9 20.5 %collective-permute-start.1 = (bf16[192,1024]{0,1:T(8,128)(2,1)}, bf16[192,1024]{0,1:T(8,128)(2,1)}, u32[]{:S(2)}, u32[]{:S(2)}) collective-permute-start(bf16[192,1024]{0,1:T(8,128)(2,1)} %fusion.138), channel_id=1, source_target_pairs={{1,0},{2,1},{3,2},{4,3},{5,4},{6,5},{7,6},{8,7},{9,8},{10,9},{11,1... | collective-permute-start | bytes 1179656 | tf_op jit(solution)/shard_map/while/body/eval_jaxpr/ppermute | solution.py:17
  1735.7 3.2 copy-start.15
Sparse Core Ops, SparseCore 0:
  320.5 66.7 all-reduce.6
  390.3 1345.3 all-reduce.4
